TPU v7x, 128 devices: a whole 4x4x4 slice. The times are simulated.
128 devices in a mesh: seq: 16 (over z_lo, y, core), head: 8 (over x, z_hi).
Axes of the slice: x: 4, y: 4, z: 4 (z_hi: 2, z_lo: 2; z = z_hi * 2 + z_lo), core: 2. Of those that a mesh axis runs over, the one named last changes fastest.
Arguments:
- frames: bfloat16 [8192, 2048], P('seq')
- w_query: bfloat16 [2048, 2048], P(None, 'head'), may hold values from -0.125 to 0.125
- w_key: bfloat16 [2048, 2048], P(None, 'head'), may hold values from -0.125 to 0.125
- w_value: bfloat16 [2048, 2048], P(None, 'head'), may hold values from -0.125 to 0.125
- w_out: bfloat16 [2048, 2048], P('head'), may hold values from -1 to 1
- conv_taps: float32 [31, 2048], P(None, 'head'), may hold values from -1 to 1
- conv_bias: float32 [2048], P('head'), may hold values from -1 to 1
- norm_gain: float32 [2048], replicated, may hold values from 0.5 to 1.5
- w_up: bfloat16 [2048, 8192], P(None, 'head'), may hold values from -0.125 to 0.125
- w_down: bfloat16 [8192, 2048], P('head'), may hold values from -0.0625 to 0.0625
- block_lists: int32 [64, 8], P('seq'), may hold values from 0 to 63, as said below
- block_counts: int32 [64], P('seq'), may hold values from 1 to 8, as said below
Outputs:
- layer_out: bfloat16 [8192, 2048], P('seq', 'head')
Inputs may be any that keep to these rules, and one draw needn't show every extreme that they name: `block_lists`: entry 0 of query block b's list is b itself; the 8 entries of a list are distinct block indices. `block_counts`: query block 0 has all 8 entries active.
All inputs are finite; a program needn't handle non-finite values.
Results may differ from a plain program's by a relative error of at most 0.02.
The roundings to bfloat16 on the way count: a program that leaves them out, or rounds other values in their place, can miss the bound.
Values may be sent and summed in bfloat16 or wider, within the bound.
A program may use at most 128 MiB of HBM per device.

v0:
```python
import math
import jax
import jax.numpy as jnp
from jax import lax
from jax.sharding import PartitionSpec as P

HD = 64
KERNEL = 31


def extended(cells, sides, width):
    for axis, dim in sides:
        count = lax.axis_size(axis)
        ends = count - 1
        head = lax.slice_in_dim(cells, 0, width, axis=dim)
        tail = lax.slice_in_dim(cells, cells.shape[dim] - width, cells.shape[dim], axis=dim)
        cells = jnp.concatenate(
            [
                lax.ppermute(tail, axis, [(i, (i + 1) % count) for i in range(ends)]),
                cells,
                lax.ppermute(head, axis, [((i + 1) % count, i) for i in range(ends)]),
            ],
            axis=dim,
        )
    return cells


def on_device(
    frames,
    w_query,
    w_key,
    w_value,
    w_out,
    conv_taps,
    conv_bias,
    norm_gain,
    w_up,
    w_down,
    block_lists,
    block_counts,
):
    frame_rows = frames.shape[0]
    width_dev = w_query.shape[1]
    heads_dev = width_dev // HD
    query_blocks = block_lists.shape[0]
    block_rows = frame_rows // query_blocks
    total_blocks = query_blocks * lax.axis_size("seq")
    query = jnp.dot(frames, w_query, preferred_element_type=jnp.float32).astype(jnp.bfloat16)
    keys = jnp.dot(frames, w_key, preferred_element_type=jnp.float32).astype(jnp.bfloat16)
    values = jnp.dot(frames, w_value, preferred_element_type=jnp.float32).astype(jnp.bfloat16)
    slot_live = jnp.arange(block_lists.shape[1])[None, :] < block_counts[:, None]
    hits = (block_lists[:, :, None] == jnp.arange(total_blocks)[None, None, :]) & slot_live[
        :, :, None
    ]
    table = jnp.sum(hits.astype(jnp.float32), axis=1)
    query_heads = query.reshape(frame_rows, heads_dev, HD)
    stacked = jnp.stack([keys, values])

    def allowed_of(key_start, count):
        key_block = (key_start + jnp.arange(count)) // block_rows
        onehot = (key_block[:, None] == jnp.arange(total_blocks)[None, :]).astype(jnp.float32)
        coarse = jnp.dot(table, onehot.T)
        return jnp.repeat(coarse, block_rows, axis=0) > 0.5

    def update(carry, key_part, value_part, allowed):
        run_max, run_sum, run_acc = carry
        count = key_part.shape[0]
        key_heads = key_part.reshape(count, heads_dev, HD)
        value_heads = value_part.reshape(count, heads_dev, HD)
        scores = (
            jnp.einsum("qhd,khd->hqk", query_heads, key_heads, preferred_element_type=jnp.float32)
            * 0.125
        )
        scores = jnp.where(allowed[None], scores, -1e30)
        new_max = jnp.maximum(run_max, jnp.max(scores, axis=2))
        probs = jnp.where(allowed[None], jnp.exp(scores - new_max[:, :, None]), 0.0)
        rescale = jnp.exp(run_max - new_max)
        new_sum = run_sum * rescale + jnp.sum(probs, axis=2)
        new_acc = run_acc * rescale[:, :, None] + jnp.einsum(
            "hqk,khd->hqd",
            probs.astype(jnp.bfloat16),
            value_heads,
            preferred_element_type=jnp.float32,
        )
        return (new_max, new_sum, new_acc)

    start_state = (
        jnp.full((heads_dev, frame_rows), -1e30, jnp.float32),
        jnp.zeros((heads_dev, frame_rows), jnp.float32),
        jnp.zeros((heads_dev, frame_rows, HD), jnp.float32),
    )
    carry = start_state
    piece = lax.all_gather(stacked, "seq", axis=1, tiled=True)
    count = piece.shape[1]
    step_rows = math.gcd(count, 512)
    turns = count // step_rows
    parts = piece.reshape(2, turns, step_rows, width_dev).swapaxes(0, 1)
    offsets = step_rows * jnp.arange(turns)

    def visit(inner, item):
        part, offset = item
        allowed = allowed_of(offset, step_rows)
        inner = update(inner, part[0], part[1], allowed)
        return (inner, None)

    carry, _ = lax.scan(visit, carry, (parts, offsets))
    run_max, run_sum, run_acc = carry
    attended = (
        (run_acc / run_sum[:, :, None])
        .transpose(1, 0, 2)
        .reshape(frame_rows, width_dev)
        .astype(jnp.bfloat16)
    )
    columns = w_out
    mixed = lax.psum_scatter(
        jnp.einsum("fk,kc->cf", attended, columns, preferred_element_type=jnp.float32).astype(
            jnp.bfloat16
        ),
        "head",
        scatter_dimension=0,
        tiled=True,
    ).astype(jnp.float32)
    own_start = lax.axis_index("head") * width_dev
    residual_in = lax.dynamic_slice_in_dim(frames, own_start, width_dev, 1).T.astype(jnp.float32)
    stream = (residual_in + mixed).astype(jnp.bfloat16)
    padded = extended(stream, (("seq", 1),), KERNEL // 2).astype(jnp.float32)
    conv_sum = jnp.zeros((width_dev, frame_rows), jnp.float32)
    for tap in range(KERNEL):
        conv_sum = conv_sum + conv_taps[tap][:, None] * padded[:, tap : tap + frame_rows]
    second = (stream.astype(jnp.float32) + jax.nn.silu(conv_sum + conv_bias[:, None])).astype(
        jnp.bfloat16
    )
    whole = lax.all_gather(second, "head", axis=0, tiled=True).astype(jnp.float32)
    mean = jnp.mean(whole, axis=0, keepdims=True)
    centered = whole - mean
    var = jnp.mean(centered * centered, axis=0, keepdims=True)
    normed = (centered * lax.rsqrt(var + 1e-05) * norm_gain[:, None]).astype(jnp.bfloat16)
    upper = jnp.einsum("df,dk->fk", normed, w_up, preferred_element_type=jnp.float32)
    hidden = jax.nn.silu(upper).astype(jnp.bfloat16)
    columns = w_down
    ffsum = lax.psum_scatter(
        jnp.einsum("fk,kc->cf", hidden, columns, preferred_element_type=jnp.float32).astype(
            jnp.bfloat16
        ),
        "head",
        scatter_dimension=0,
        tiled=True,
    ).astype(jnp.float32)
    return (second.astype(jnp.float32) + ffsum).astype(jnp.bfloat16).T


def solution(mesh):
    placed = (
        P("seq", None),
        P(None, "head"),
        P(None, "head"),
        P(None, "head"),
        P("head", None),
        P(None, "head"),
        P("head"),
        P(),
        P(None, "head"),
        P("head", None),
        P("seq", None),
        P("seq"),
    )
    return jax.shard_map(
        on_device, mesh=mesh, in_specs=placed, out_specs=P("seq", "head"), check_vma=False
    )
```

profile of v0, /device:TPU:0, one launch (start us, length us, event | category | flops | bytes accessed | tf_op | source)
XLA Modules:
  0.0 521.4 jit_solution(5680154871138046375)
XLA Ops:
  6.6 2.7 fusion.32
  9.3 2.6 fusion.33
  13.0 2.3 convolution_convert_fusion.2
  15.4 52.2 %all-gather.3.cloned.1.call-done = bf16[2,8192,256]{2,1,0:T(8,128)(2,1)} async-done(((bf16[2,512,256]{2,1,0:T(8,128)(2,1)}), bf16[2,8192,256]{2,1,0:T(8,128)(2,1)}) %all-gather.3.cloned.1.call-update) | async-done | bytes 8388624 | tf_op jit(solution)/shard_map/all_gather | solution.py:93
  67.5 12.3 %copy.18 = bf16[2,16,512,256]{2,3,0,1:T(8,128)(2,1)} copy(bf16[2,16,512,256]{3,2,1,0:T(8,128)(2,1)} %bitcast.121) | data formatting | bytes 16777216 | tf_op jit(solution)/shard_map/reshape | solution.py:97
  79.9 196.1 %while.17 = (s32[]{:T(128)}, f32[4,512]{1,0:T(4,128)S(1)}, f32[4,512]{1,0:T(4,128)S(1)}, f32[4,512,64]{1,2,0:T(8,128)S(1)}, s32[16]{0:T(128)S(1)}, /*index=5*/bf...) while((s32[]{:T(128)}, f32[4,512]{1,0:T(4,128)S(1)}, ...), condition=%wide.region_4.5_spmd.clone, body=%wide.region_1.4_spmd.clone.sunk | while | flops 282775552 | bytes 33960632 | solution.py:106
  84.4 2.9 fusion.104
  87.3 3.4 fusion.105
  96.7 2.9 fusion.104
  99.5 3.4 fusion.105
  108.9 2.9 fusion.104
  111.8 3.4 fusion.105
  121.2 2.9 fusion.104
  124.0 3.4 fusion.105
  133.4 2.9 fusion.104
  136.3 3.4 fusion.105
  145.7 2.9 fusion.104
  148.6 3.4 fusion.105
  157.9 2.9 fusion.104
  160.8 3.4 fusion.105
  170.2 2.9 fusion.104
  173.1 3.4 fusion.105
  182.4 2.9 fusion.104
  185.3 3.4 fusion.105
  194.7 2.9 fusion.104
  197.6 3.4 fusion.105
  207.0 2.9 fusion.104
  209.8 3.4 fusion.105
  219.2 2.9 fusion.104
  222.1 3.4 fusion.105
  231.5 2.9 fusion.104
  234.3 3.4 fusion.105
  243.7 2.9 fusion.104
  246.6 3.4 fusion.105
  256.0 2.9 fusion.104
  258.8 3.4 fusion.105
  268.2 2.9 fusion.104
  271.1 3.4 fusion.105
  276.0 2.1 fusion.23
  278.2 76.4 %reduce-scatter.3.cloned.1.call-done = bf16[256,512]{0,1:T(8,128)(2,1)} async-done(((bf16[2048,512]{0,1:T(8,128)(2,1)}), bf16[256,512]{0,1:T(8,128)(2,1)}) %reduce-scatter.3.cloned.1.call-update) | async-done | bytes 262160 | tf_op jit(solution)/shard_map/reduce_scatter | solution.py:115
  358.4 3.5 collective-permute-done.1
  361.9 2.9 add_convert_fusion.1
  365.1 59.7 %all-gather.5.cloned.1.call-done = bf16[2048,512]{0,1:T(8,128)(2,1)} async-done(((bf16[256,512]{0,1:T(8,128)(2,1)}), bf16[2048,512]{0,1:T(8,128)(2,1)}) %all-gather.5.cloned.1.call-update) | async-done | bytes 2097168 | tf_op jit(solution)/shard_map/all_gather | solution.py:133
  424.8 2.1 convert_reduce_fusion
  426.9 2.3 fusion.20
  429.2 9.6 %fusion.24 = bf16[2048,512]{0,1:T(8,128)(2,1)} fusion(bf16[1024,2048]{1,0:T(8,128)(2,1)} %param.23, bf16[2048,1024]{1,0:T(8,128)(2,1)} %param.22, bf16[2048,512]{0,1:T(8,128)(2,1)S(1)} %copy-done.2, f32[2048]{0:T(1024)S(1)} %copy-done.8, f32[512]{0:T(512)S(1)} %add_rsqrt_fusion, f32[512]{0:T(512)S(1)} %broadcast_multiply_fusion), kind=kOutput, calls=%fused_computation.42 | convolution fusion | flops 4303880192 | bytes 12595200 | tf_op jit(solution)/shard_map/fk,kc->cf/dot_general | solution.py:142
  438.9 74.3 %reduce-scatter.5.cloned.1.call-done = bf16[256,512]{0,1:T(8,128)(2,1)} async-done(((bf16[2048,512]{0,1:T(8,128)(2,1)}), bf16[256,512]{0,1:T(8,128)(2,1)}) %reduce-scatter.5.cloned.1.call-update) | async-done | bytes 262160 | tf_op jit(solution)/shard_map/reduce_scatter | solution.py:141
  513.1 1.7 fusion.68
  (252 shorter events, 100.2 us)
Async XLA Ops:
  6.5 269.5 %copy-start = (bf16[256,2048]{1,0:T(8,128)(2,1)S(1)}, bf16[256,2048]{1,0:T(8,128)(2,1)}, u32[]{:S(2)}) copy-start(bf16[256,2048]{1,0:T(8,128)(2,1)} %param.18) | copy-start | bytes 3145732
  6.5 6.3 %copy-start.9 = (s32[4]{0:T(128)S(1)}, s32[4]{0:T(128)}, u32[]{:S(2)}) copy-start(s32[4]{0:T(128)} %param.25) | copy-start | bytes 52
  6.5 6.4 %copy-start.5 = (s32[4,8]{1,0:T(4,128)S(1)}, s32[4,8]{1,0:T(4,128)}, u32[]{:S(2)}) copy-start(s32[4,8]{1,0:T(4,128)} %param.24) | copy-start | bytes 388
  6.5 6.5 %copy-start.7 = (bf16[2048,256]{1,0:T(8,128)(2,1)S(1)}, bf16[2048,256]{1,0:T(8,128)(2,1)}, u32[]{:S(2)}) copy-start(bf16[2048,256]{1,0:T(8,128)(2,1)} %param.15) | copy-start | bytes 3145732
  6.5 61.0 %all-gather.3.cloned.1.call-start = ((), (), s32[]{:S(2)}) async-start(), calls=%async_computation.2 | async-start | bytes 8912896 | tf_op jit(solution)/shard_map/all_gather | solution.py:93
  12.7 341.9 %reduce-scatter.3.cloned.1.call-start = ((), (), s32[]{:S(2)}) async-start(), calls=%async_computation.3 | async-start | bytes 2359296 | tf_op jit(solution)/shard_map/reduce_scatter | solution.py:115
  87.3 3.4 copy-start.1
  99.5 3.4 copy-start.1
  111.8 3.4 copy-start.1
  124.0 3.4 copy-start.1
  136.3 3.4 copy-start.1
  148.5 3.4 copy-start.1
  160.8 3.4 copy-start.1
  173.1 3.4 copy-start.1
  185.3 3.4 copy-start.1
  197.6 3.4 copy-start.1
  209.8 3.4 copy-start.1
  222.1 3.4 copy-start.1
  234.3 3.4 copy-start.1
  246.6 3.4 copy-start.1
  258.8 3.4 copy-start.1
  271.1 3.4 copy-start.1
  275.9 2.3 copy-start.4
  276.0 85.9 %copy-start.6 = (f32[256]{0:T(256)S(1)}, f32[256]{0:T(256)}, u32[]{:S(2)}) copy-start(f32[256]{0:T(256)} %param.20) | copy-start | bytes 3076
  278.1 146.7 %all-gather.5.cloned.1.call-start = ((), (), s32[]{:S(2)}) async-start(), calls=%async_computation.4 | async-start | bytes 2359296 | tf_op jit(solution)/shard_map/all_gather | solution.py:133
  355.7 2.6 collective-permute-start
  357.0 4.8 collective-permute-start.1
  364.8 64.4 %copy-start.8 = (f32[2048]{0:T(1024)S(1)}, f32[2048]{0:T(1024)}, u32[]{:S(2)}) copy-start(f32[2048]{0:T(1024)} %param.21) | copy-start | bytes 24580
  364.9 148.2 %reduce-scatter.5.cloned.1.call-start = ((), (), s32[]{:S(2)}) async-start(), calls=%async_computation.5 | async-start | bytes 2359296 | tf_op jit(solution)/shard_map/reduce_scatter | solution.py:141
  424.8 4.4 copy-start.2
  429.2 83.9 %copy-start.3 = (bf16[256,512]{0,1:T(8,128)(2,1)S(1)}, bf16[256,512]{0,1:T(8,128)(2,1)}, u32[]{:S(2)}) copy-start(bf16[256,512]{0,1:T(8,128)(2,1)} %add_convert_fusion.1) | copy-start | bytes 786436
Sparse Core Ops, SparseCore 0:
  12.9 54.6 all-gather.2
  278.2 76.3 reduce-scatter.2
  365.0 59.8 all-gather.4
  439.0 74.0 reduce-scatter.4
where the time goes:
time: 522 us; the launch traced here: 521 us
  waiting for transfers between devices  266 us (51%)
  matrix products  90.8 us (17%)
  other arithmetic  75.9 us (15%)
  local copies, waits for them, and re-layouts  71.2 us (14%)
  between operations  13.3 us (3%)
    reduce_scatter x1, waiting for transfers between devices, on_device(): lax.psum_scatter(jnp.einsum('fk,kc->cf', attended, columns, preferred_ele...  76.4 us
    reduce_scatter x1, waiting for transfers between devices, on_device(): lax.psum_scatter(jnp.einsum('fk,kc->cf', hidden, columns, preferred_eleme...  74.3 us
    all_gather x1, waiting for transfers between devices, on_device(): lax.all_gather(second, 'head', axis=0, tiled=True).astype(jnp.float32)  59.7 us
    reduce_sum x16, other arithmetic, update(): new_sum = run_sum * rescale + jnp.sum(probs, axis=2)  54.2 us
    all_gather x1, waiting for transfers between devices, on_device(): piece = lax.all_gather(stacked, 'seq', axis=1, tiled=True)  52.2 us
    dot_general x16, matrix products, update(): jnp.einsum('qhd,khd->hqk', query_heads, key_heads, preferred_element_type...  45.9 us
    broadcast_in_dim x16, local copies, waits for them, and re-layouts, allowed_of(): return jnp.repeat(coarse, block_rows, axis=0) > 0.5  25.6 us
    dot_general x16, matrix products, update(): jnp.einsum('hqk,khd->hqd', probs.astype(jnp.bfloat16), value_heads, prefe...  21.6 us
  transfers between devices with their start and end apart: 6, of which 5 were waited for; matrix products, arithmetic and copies ran while one was open for 0% of the time, Pallas kernels for 0%

commit v1 on v0

--- a/solution.py
+++ b/solution.py
@@ -6,6 +6,11 @@
 
 HD = 64
 KERNEL = 31
+
+
+def swapped_in(array, name, dim):
+    sent = jnp.stack([array] * lax.axis_size(name))
+    return jnp.concatenate(lax.all_to_all(sent, name, 0, 0), axis=dim)
 
 
 def extended(cells, sides, width):
@@ -130,7 +135,7 @@
     second = (stream.astype(jnp.float32) + jax.nn.silu(conv_sum + conv_bias[:, None])).astype(
         jnp.bfloat16
     )
-    whole = lax.all_gather(second, "head", axis=0, tiled=True).astype(jnp.float32)
+    whole = swapped_in(second, "head", 0).astype(jnp.float32)
     mean = jnp.mean(whole, axis=0, keepdims=True)
     centered = whole - mean
     var = jnp.mean(centered * centered, axis=0, keepdims=True)

time: 522 us -> 493 us (0.944)
  waiting for transfers between devices: 266 us -> 208 us
  blocking collectives: 0 us -> 31.3 us
    all_gather x1 -> x0, waiting for transfers between devices: 59.7 us -> none  [on_device(): lax.all_gather(second, 'head', axis=0, tiled=True).astype(jnp.float32)]
    all_to_all x0 -> x1, blocking collectives: none -> 31.3 us  [swapped_in(): return jnp.concatenate(lax.all_to_all(sent, name, 0, 0), axis=dim)]
  transfers between devices with their start and end apart: 6 -> 5, of which waited for: 5 -> 4; matrix products, arithmetic and copies ran while one was open for 0% -> 1% of each run, Pallas kernels for 0% -> 0%
where the time goes in v1:
time: 493 us; the launch traced here: 492 us
  waiting for transfers between devices  208 us (42%)
  matrix products  90.9 us (18%)
  other arithmetic  72.5 us (15%)
  local copies, waits for them, and re-layouts  71.6 us (15%)
  blocking collectives  31.3 us (6%)
  between operations  13.3 us (3%)
    reduce_scatter x1, waiting for transfers between devices, on_device(): lax.psum_scatter(jnp.einsum('fk,kc->cf', attended, columns, preferred_ele...  76.4 us
    reduce_scatter x1, waiting for transfers between devices, on_device(): lax.psum_scatter(jnp.einsum('fk,kc->cf', hidden, columns, preferred_eleme...  76.2 us
    reduce_sum x16, other arithmetic, update(): new_sum = run_sum * rescale + jnp.sum(probs, axis=2)  54.2 us
    all_gather x1, waiting for transfers between devices, on_device(): piece = lax.all_gather(stacked, 'seq', axis=1, tiled=True)  52.2 us
    dot_general x16, matrix products, update(): jnp.einsum('qhd,khd->hqk', query_heads, key_heads, preferred_element_type...  45.7 us
    all_to_all x1, blocking collectives, swapped_in(): return jnp.concatenate(lax.all_to_all(sent, name, 0, 0), axis=dim)  31.3 us
    broadcast_in_dim x16, local copies, waits for them, and re-layouts, allowed_of(): return jnp.repeat(coarse, block_rows, axis=0) > 0.5  25.6 us
    dot_general x16, matrix products, update(): jnp.einsum('hqk,khd->hqd', probs.astype(jnp.bfloat16), value_heads, prefe...  21.9 us
  transfers between devices with their start and end apart: 5, of which 4 were waited for; matrix products, arithmetic and copies ran while one was open for 1% of the time, Pallas kernels for 0%

profile of v1, /device:TPU:0, one launch (start us, length us, event | category | flops | bytes accessed | tf_op | source)
XLA Modules:
  0.0 491.6 jit_solution(12425076827189549539)
XLA Ops:
  6.6 2.7 fusion.23
  9.3 2.6 fusion.24
  13.0 2.4 convolution_convert_fusion.2
  15.4 52.2 %all-gather.2.cloned.1.call-done = bf16[2,8192,256]{2,1,0:T(8,128)(2,1)} async-done(((bf16[2,512,256]{2,1,0:T(8,128)(2,1)}), bf16[2,8192,256]{2,1,0:T(8,128)(2,1)}) %all-gather.2.cloned.1.call-update) | async-done | bytes 8388624 | tf_op jit(solution)/shard_map/all_gather | solution.py:98
  67.5 12.3 %copy.19 = bf16[2,16,512,256]{2,3,0,1:T(8,128)(2,1)} copy(bf16[2,16,512,256]{3,2,1,0:T(8,128)(2,1)} %bitcast.130) | data formatting | bytes 16777216 | tf_op jit(solution)/shard_map/reshape | solution.py:102
  79.8 196.2 %while.17 = (s32[]{:T(128)}, f32[4,512]{1,0:T(4,128)S(1)}, f32[4,512]{1,0:T(4,128)S(1)}, f32[4,512,64]{1,2,0:T(8,128)S(1)}, s32[16]{0:T(128)S(1)}, /*index=5*/bf...) while((s32[]{:T(128)}, f32[4,512]{1,0:T(4,128)S(1)}, ...), condition=%wide.region_4.5_spmd.clone, body=%wide.region_1.4_spmd.clone.sunk | while | flops 282775552 | bytes 33960632 | solution.py:111
  81.6 1.6 broadcast_in_dim.102
  84.4 2.9 fusion.97
  87.3 3.4 fusion.98
  96.7 2.9 fusion.97
  99.5 3.4 fusion.98
  106.1 1.6 broadcast_in_dim.102
  108.9 2.9 fusion.97
  111.8 3.4 fusion.98
  121.2 2.9 fusion.97
  124.1 3.4 fusion.98
  133.4 2.9 fusion.97
  136.3 3.4 fusion.98
  145.7 2.9 fusion.97
  148.6 3.4 fusion.98
  158.0 2.9 fusion.97
  160.8 3.4 fusion.98
  170.2 2.9 fusion.97
  173.1 3.4 fusion.98
  182.5 2.9 fusion.97
  185.4 3.4 fusion.98
  194.8 2.9 fusion.97
  197.6 3.4 fusion.98
  207.0 2.9 fusion.97
  209.9 3.4 fusion.98
  219.3 2.9 fusion.97
  222.2 3.4 fusion.98
  231.6 2.9 fusion.97
  234.4 3.4 fusion.98
  243.8 2.9 fusion.97
  246.7 3.4 fusion.98
  256.1 2.9 fusion.97
  259.0 3.4 fusion.98
  268.3 2.9 fusion.97
  271.2 3.4 fusion.98
  276.1 2.1 fusion.21
  278.3 76.4 %reduce-scatter.3.cloned.1.call-done = bf16[256,512]{0,1:T(8,128)(2,1)} async-done(((bf16[2048,512]{0,1:T(8,128)(2,1)}), bf16[256,512]{0,1:T(8,128)(2,1)}) %reduce-scatter.3.cloned.1.call-update) | async-done | bytes 262160 | tf_op jit(solution)/shard_map/reduce_scatter | solution.py:120
  358.4 3.5 collective-permute-done.1
  362.0 2.3 add_convert_fusion.1
  364.6 31.3 %all_to_all.5 = bf16[8,256,512]{2,1,0:T(8,128)(2,1)S(1)} all-to-all(bf16[8,256,512]{2,1,0:T(8,128)(2,1)S(1)} %stack.11), channel_id=1, replica_groups=mesh['seq'=16,'head'=8] {'head'}, dimensions={0} | all-to-all | bytes 4194304 | tf_op jit(solution)/shard_map/all_to_all | solution.py:13
  397.5 9.6 %fusion.22 = bf16[2048,512]{0,1:T(8,128)(2,1)} fusion(bf16[1024,2048]{1,0:T(8,128)(2,1)} %param.23, bf16[2048,512]{1,0:T(8,128)(2,1)S(1)} %fusion.20, bf16[2048,1024]{1,0:T(8,128)(2,1)} %param.22), kind=kOutput, calls=%fused_computation.40 | convolution fusion | flops 4298637312 | bytes 12582912 | tf_op jit(solution)/shard_map/fk,kc->cf/dot_general | solution.py:147
  407.1 76.2 %reduce-scatter.5.cloned.1.call-done = bf16[256,512]{0,1:T(8,128)(2,1)} async-done(((bf16[2048,512]{0,1:T(8,128)(2,1)}), bf16[256,512]{0,1:T(8,128)(2,1)}) %reduce-scatter.5.cloned.1.call-update) | async-done | bytes 262160 | tf_op jit(solution)/shard_map/reduce_scatter | solution.py:146
  483.4 1.7 fusion.58
  (249 shorter events, 99.0 us)
Async XLA Ops:
  6.5 269.6 %copy-start = (bf16[256,2048]{1,0:T(8,128)(2,1)S(1)}, bf16[256,2048]{1,0:T(8,128)(2,1)}, u32[]{:S(2)}) copy-start(bf16[256,2048]{1,0:T(8,128)(2,1)} %param.18) | copy-start | bytes 3145732
  6.5 6.3 %copy-start.7 = (s32[4]{0:T(128)S(1)}, s32[4]{0:T(128)}, u32[]{:S(2)}) copy-start(s32[4]{0:T(128)} %param.25) | copy-start | bytes 52
  6.5 6.4 %copy-start.4 = (s32[4,8]{1,0:T(4,128)S(1)}, s32[4,8]{1,0:T(4,128)}, u32[]{:S(2)}) copy-start(s32[4,8]{1,0:T(4,128)} %param.24) | copy-start | bytes 388
  6.5 6.5 %copy-start.6 = (bf16[2048,256]{1,0:T(8,128)(2,1)S(1)}, bf16[2048,256]{1,0:T(8,128)(2,1)}, u32[]{:S(2)}) copy-start(bf16[2048,256]{1,0:T(8,128)(2,1)} %param.15) | copy-start | bytes 3145732
  6.5 61.0 %all-gather.2.cloned.1.call-start = ((), (), s32[]{:S(2)}) async-start(), calls=%async_computation.3 | async-start | bytes 8912896 | tf_op jit(solution)/shard_map/all_gather | solution.py:98
  12.7 342.0 %reduce-scatter.3.cloned.1.call-start = ((), (), s32[]{:S(2)}) async-start(), calls=%async_computation.4 | async-start | bytes 2359296 | tf_op jit(solution)/shard_map/reduce_scatter | solution.py:120
  87.2 3.4 copy-start.1
  99.5 3.4 copy-start.1
  111.8 3.4 copy-start.1
  124.0 3.4 copy-start.1
  136.3 3.4 copy-start.1
  148.6 3.4 copy-start.1
  160.8 3.4 copy-start.1
  173.1 3.4 copy-start.1
  185.4 3.4 copy-start.1
  197.6 3.4 copy-start.1
  209.9 3.4 copy-start.1
  222.2 3.4 copy-start.1
  234.4 3.4 copy-start.1
  246.7 3.4 copy-start.1
  258.9 3.4 copy-start.1
  271.2 3.4 copy-start.1
  276.0 2.3 copy-start.2
  276.1 85.8 %copy-start.5 = (f32[256]{0:T(256)S(1)}, f32[256]{0:T(256)}, u32[]{:S(2)}) copy-start(f32[256]{0:T(256)} %param.20) | copy-start | bytes 3076
  278.3 205.1 %reduce-scatter.5.cloned.1.call-start = ((), (), s32[]{:S(2)}) async-start(), calls=%async_computation.5 | async-start | bytes 2359296 | tf_op jit(solution)/shard_map/reduce_scatter | solution.py:146
  355.8 2.6 collective-permute-start
  357.1 4.8 collective-permute-start.1
  364.6 32.3 %copy-start.3 = (f32[2048]{0:T(1024)S(1)}, f32[2048]{0:T(1024)}, u32[]{:S(2)}) copy-start(f32[2048]{0:T(1024)} %param.21) | copy-start | bytes 24580
Sparse Core Ops, SparseCore 0:
  12.8 54.6 all-gather.1
  278.4 76.2 reduce-scatter.2
  407.2 76.0 reduce-scatter.4
